TPU v7x, 32 devices: a whole 2x2x4 slice. The times are simulated.
32 devices in a mesh: groups: 2 (over y), text: 4 (over z), image: 4 (over x, core).
Axes of the slice: x: 2, y: 2, z: 4, core: 2. Of those that a mesh axis runs over, the one named last changes fastest.
Arguments:
- text_states: bfloat16 [1024, 8192], P(('groups', 'text')), parts along dimension 0, may hold values from -6 to 6
- grid_levels: bfloat16 [16384, 8192], P(('groups', 'text'), 'image'), parts along dimension 0, may hold values from -8 to 7, as said below
- round_logits: float32 [16384, 8192], P(('groups', 'text'), 'image'), parts along dimension 0, may hold values from -2 to 2
- column_steps: float32 [16384], P(('groups', 'image')), parts along dimension 0, may hold values from 0.0015 to 0.004
- image_keys: bfloat16 [12808, 1024], P('groups', 'image'), parts along dimension 0, may hold values from -500 to 500
- image_values: bfloat16 [12808, 1024], P('groups', 'image'), parts along dimension 0, may hold values from -6 to 6
- target_out: bfloat16 [1024, 8192], P(('groups', 'text'), 'image'), parts along dimension 0, may hold values from -6 to 6
- doc_images: int32 [6], P('groups'), parts along dimension 0, may hold values from 1 to 2, as said below
- image_start: int32 [8], P('groups'), parts along dimension 0, may hold values from 1 to 3, as said below
Outputs:
- rounding_grad: float32 [16384, 8192], P(('groups', 'text'), 'image'), parts along dimension 0
There are 2 independent parts, one for each index of `groups`. A program takes and returns all parts, laid end to end along the dimension named above; each array names one. Nothing has to cross between parts.
Inputs may be any that keep to these rules, and one draw needn't show every extreme that they name: `doc_images`: every document holds one image or more, 4 in all; one document holds exactly 2, and no document more. `image_start`: Nondecreasing; the first image's entry is 1 and the last image's 4 - 1. `grid_levels`: whole numbers.
All inputs are finite; a program needn't handle non-finite values.
Results may differ from a plain program's by a relative error of at most 0.015.
Values may be sent and summed in bfloat16 or wider, within the bound.
A program may use at most 256 MiB of HBM per device.

v0:
```python
import jax
import jax.numpy as jnp
from jax import lax
from jax.sharding import PartitionSpec as P

H = 64
KVH = 8
HD = 128
IMAGES = 4
IMG_TOK = 1601
SPAN = 128


def visibility(span_ids, doc_images, image_start, total_spans):
    images = image_start.shape[0]
    documents = doc_images.shape[0]
    doc_ends = jnp.cumsum(doc_images)
    positions = jnp.arange(images, dtype=jnp.int32)
    doc_of = jnp.sum((positions[:, None] >= doc_ends[None, :]).astype(jnp.int32), axis=1)
    doc_index = jnp.arange(documents, dtype=jnp.int32)
    end_of = jnp.sum(jnp.where(doc_index[None, :] == doc_of[:, None], doc_ends[None, :], 0), axis=1)
    stop_at = jnp.sum(
        jnp.where(positions[None, :] == end_of[:, None], image_start[None, :], 0), axis=1
    )
    stop_at = stop_at + jnp.where(end_of >= images, total_spans, 0)
    return (span_ids[:, None] >= image_start[None, :]) & (span_ids[:, None] < stop_at[None, :])


def head_grad(queries, keys, values, target, visible):
    tokens_here = queries.shape[0]
    kv_heads = queries.shape[1]
    per_group = queries.shape[2]
    head_size = queries.shape[3]
    scaling = head_size ** (-0.5)
    shape = (kv_heads, per_group, tokens_here)

    def tile_of(which):
        keys_now = lax.dynamic_slice_in_dim(keys, which * IMG_TOK, IMG_TOK, 0)
        values_now = lax.dynamic_slice_in_dim(values, which * IMG_TOK, IMG_TOK, 0)
        scores = (
            jnp.einsum("tkgd,nkd->kgtn", queries, keys_now, preferred_element_type=jnp.float32)
            * scaling
        )
        return (scores, keys_now, values_now)

    def seen_of(which):
        return lax.dynamic_index_in_dim(visible, which, 1, keepdims=False)

    def forward(which, state):
        seen_rows = seen_of(which)
        running, total, accum = state
        scores, keys_now, values_now = tile_of(which)
        seen = seen_rows[None, None, :]
        peak = jnp.where(seen, jnp.maximum(running, jnp.max(scores, axis=-1)), running)
        weights = jnp.where(seen[..., None], jnp.exp(scores - peak[..., None]), 0.0)
        fade = jnp.exp(running - peak)
        total = total * fade + jnp.sum(weights, axis=-1)
        product = jnp.einsum(
            "kgtn,nkd->kgtd",
            weights.astype(jnp.bfloat16),
            values_now,
            preferred_element_type=jnp.float32,
        )
        return (peak, total, accum * fade[..., None] + product)

    start_state = (
        jnp.full(shape, -1e30, jnp.float32),
        jnp.zeros(shape, jnp.float32),
        jnp.zeros(shape + (head_size,), jnp.float32),
    )
    running, total, accum = lax.fori_loop(0, IMAGES, forward, start_state)
    denom = jnp.maximum(total, 1.0)
    attended = accum / denom[..., None]
    out_grad = (1024.0 * (attended - target)).astype(jnp.bfloat16)
    delta = jnp.sum(out_grad.astype(jnp.float32) * attended, axis=-1)

    def backward(which, grad_acc):
        seen_rows = seen_of(which)
        scores, keys_now, values_now = tile_of(which)
        seen = seen_rows[None, None, :]
        probs = (
            jnp.where(seen[..., None], jnp.exp(scores - running[..., None]), 0.0) / denom[..., None]
        )
        dprob = jnp.einsum(
            "kgtd,nkd->kgtn", out_grad, values_now, preferred_element_type=jnp.float32
        )
        score_grad = (probs * (dprob - delta[..., None]) * scaling).astype(jnp.bfloat16)
        return grad_acc + jnp.einsum(
            "kgtn,nkd->kgtd", score_grad, keys_now, preferred_element_type=jnp.float32
        )

    grad_sum = lax.fori_loop(0, IMAGES, backward, jnp.zeros(shape + (head_size,), jnp.float32))
    return grad_sum.astype(jnp.bfloat16)


def per_device(
    text_states,
    grid_levels,
    round_logits,
    column_steps,
    image_keys,
    image_values,
    target_out,
    doc_images,
    image_start,
):
    tok_dev = text_states.shape[0]
    out_cols = grid_levels.shape[1]
    n_text = lax.axis_size("text")
    per_group = H // KVH
    kvh_dev = image_keys.shape[1] // HD
    sigmoid_v = jax.nn.sigmoid(round_logits)
    soft = 1.2 * sigmoid_v - 0.1
    weight_q = (column_steps[None, :] * (grid_levels.astype(jnp.float32) + soft)).astype(
        jnp.bfloat16
    )
    spread = lax.all_to_all(text_states, "text", split_axis=1, concat_axis=0, tiled=True)
    q_sum = jnp.dot(
        text_states,
        lax.all_gather(weight_q, "text", axis=0, tiled=True),
        preferred_element_type=jnp.float32,
    )
    queries = q_sum.astype(jnp.bfloat16)
    first_token = lax.axis_index("text") * tok_dev
    span_ids = (first_token + jnp.arange(tok_dev, dtype=jnp.int32)) // SPAN
    visible = visibility(span_ids, doc_images, image_start, n_text * tok_dev // SPAN)
    query_tiles = queries.reshape(tok_dev, kvh_dev, per_group, HD)
    key_tiles = image_keys.reshape(image_keys.shape[0], kvh_dev, HD)
    value_tiles = image_values.reshape(image_values.shape[0], kvh_dev, HD)
    target_tiles = (
        target_out.astype(jnp.float32)
        .reshape(tok_dev, kvh_dev, per_group, HD)
        .transpose(1, 2, 0, 3)
    )
    grads = head_grad(query_tiles, key_tiles, value_tiles, target_tiles, visible)
    query_grad = grads.transpose(2, 0, 1, 3).reshape(tok_dev, out_cols)
    weight_grad = lax.dot_general(
        spread,
        lax.all_gather(query_grad, "text", axis=0, tiled=True),
        (((0,), (0,)), ((), ())),
        preferred_element_type=jnp.float32,
    )
    hprime = 1.2 * sigmoid_v * (1.0 - sigmoid_v)
    centered = 2.0 * soft - 1.0
    return (weight_grad * column_steps[None, :] - 4.0 * centered * centered * centered) * hprime


def solution(mesh):
    placed = (
        P(("groups", "text"), None),
        P(("groups", "text"), "image"),
        P(("groups", "text"), "image"),
        P(("groups", "image")),
        P("groups", "image"),
        P("groups", "image"),
        P(("groups", "text"), "image"),
        P("groups"),
        P("groups"),
    )
    return jax.shard_map(
        per_device,
        mesh=mesh,
        in_specs=placed,
        out_specs=P(("groups", "text"), "image"),
        check_vma=False,
    )
```

profile of v0, /device:TPU:0, one launch (start us, length us, event | category | flops | bytes accessed | tf_op | source)
XLA Modules:
  0.0 935.5 jit_solution(14713893510451674385)
XLA Ops:
  6.5 17.6 %copy.62 = f32[2048,2048]{0,1:T(8,128)} copy(f32[2048,2048]{1,0:T(8,128)} %param.15) | data formatting | bytes 33554432 | tf_op args[2]
  24.1 12.3 %copy.61 = bf16[2048,2048]{0,1:T(8,128)(2,1)} copy(bf16[2048,2048]{1,0:T(8,128)(2,1)} %param.14) | data formatting | bytes 16777216 | tf_op args[1]
  36.4 13.9 %multiply_convert_fusion = bf16[2048,2048]{0,1:T(8,128)(2,1)} fusion(bf16[2048,2048]{0,1:T(8,128)(2,1)} %copy.61, f32[2048]{0:T(1024)S(1)} %copy-done.6, f32[2048,2048]{0,1:T(8,128)} %copy.62), kind=kLoop, calls=%fused_computation.48 | loop fusion | flops 37748736 | bytes 33562624 | tf_op jit(solution)/shard_map/convert_element_type | solution.py:114
  52.9 6.3 all-to-all-start
  59.4 6.1 copy.63
  84.1 563.4 %all-gather.3.cloned.1.call-done = bf16[8192,2048]{0,1:T(8,128)(2,1)} async-done(((bf16[2048,2048]{0,1:T(8,128)(2,1)}), bf16[8192,2048]{0,1:T(8,128)(2,1)}) %all-gather.3.cloned.1.call-update) | async-done | bytes 33554448 | tf_op jit(solution)/shard_map/all_gather | solution.py:120
  647.5 15.9 %convolution_convert_fusion = bf16[2048,128]{1,0:T(8,128)(2,1)} fusion(bf16[8192,2048]{0,1:T(8,128)(2,1)} %all-gather.3.cloned.1.call-done, bf16[128,8192]{1,0:T(8,128)(2,1)S(1)} %copy-done), kind=kOutput, calls=%fused_computation.50 | convolution fusion | flops 4295229440 | bytes 36175872 | tf_op jit(solution)/shard_map/dot_general | solution.py:118
  664.7 94.8 %while.32 = (s32[]{:T(128)}, f32[2,8,128]{2,1,0:T(8,128)S(1)}, f32[2,8,128]{2,1,0:T(8,128)S(1)}, f32[2,8,128,128]{3,2,1,0:T(8,128)}, pred[128,4]{0,1:T(4,128)(4,...) while((s32[]{:T(128)}, f32[2,8,128]{2,1,0:T(8,128)S(1)}, ...), condition=%wide.region_7.8_spmd.clone, body=%wide.region_4.7_spmd.clone.sunk | while | flops 1712357376 | bytes 52192112 | solution.py:71
  664.9 7.8 bitcast_reduce_fusion.2
  672.8 7.3 fusion.70
  680.1 7.5 fusion.72
  688.6 7.8 bitcast_reduce_fusion.2
  696.4 7.3 fusion.70
  703.7 7.5 fusion.72
  712.2 7.8 bitcast_reduce_fusion.2
  720.0 7.3 fusion.70
  727.4 7.5 fusion.72
  735.8 7.8 bitcast_reduce_fusion.2
  743.7 7.3 fusion.70
  751.0 7.5 fusion.72
  761.7 83.7 %while.33 = (s32[]{:T(128)}, f32[2,8,128,128]{3,2,1,0:T(8,128)}, pred[128,4]{0,1:T(4,128)(4,1)S(1)}, bf16[6404,2,128]{2,0,1:T(8,128)(2,1)}, bf16[128,2,8,128]{3,...) while((s32[]{:T(128)}, f32[2,8,128,128]{3,2,1,0:T(8,128)}, ...), condition=%wide.region_10.11_spmd.clone, body=%wide.region_9.10_spmd.clone.sunk | while | flops 2544910336 | bytes 40319100 | solution.py:92
  762.0 7.8 fusion.78
  769.8 12.0 %fusion.79 = f32[2,8,128,128]{3,2,1,0:T(8,128)S(1)} fusion(f32[2,1601,128,8]{2,1,3,0:T(8,128)} %fusion.78, bf16[2,8,128,128]{3,2,1,0:T(8,128)(2,1)S(1)} %get-tuple-element.701, f32[2,8,128]{2,1,0:T(8,128)S(1)} %get-tuple-element.702, f32[2,8,128]{2,1,0:T(8,128)S(1)} %get-tuple-element.699, f32[2,8,128]{2,1,0:T(8,128)S(1)} %get-tuple-element.698, ...), kind=kOutput, calls=%fused_computation.32.clone.1 | convolution fusion | flops 1705525248 | bytes 17467008 | tf_op jit(solution)/shard_map/while/body/eval_jaxpr/kgtn,nkd->kgtd/dot_general | solution.py:88
  782.8 7.8 fusion.78
  790.7 12.0 %fusion.79 = f32[2,8,128,128]{3,2,1,0:T(8,128)S(1)} fusion(f32[2,1601,128,8]{2,1,3,0:T(8,128)} %fusion.78, bf16[2,8,128,128]{3,2,1,0:T(8,128)(2,1)S(1)} %get-tuple-element.701, f32[2,8,128]{2,1,0:T(8,128)S(1)} %get-tuple-element.702, f32[2,8,128]{2,1,0:T(8,128)S(1)} %get-tuple-element.699, f32[2,8,128]{2,1,0:T(8,128)S(1)} %get-tuple-element.698, ...), kind=kOutput, calls=%fused_computation.32.clone.1 | convolution fusion | flops 1705525248 | bytes 17467008 | tf_op jit(solution)/shard_map/while/body/eval_jaxpr/kgtn,nkd->kgtd/dot_general | solution.py:88
  803.7 7.8 fusion.78
  811.5 12.0 %fusion.79 = f32[2,8,128,128]{3,2,1,0:T(8,128)S(1)} fusion(f32[2,1601,128,8]{2,1,3,0:T(8,128)} %fusion.78, bf16[2,8,128,128]{3,2,1,0:T(8,128)(2,1)S(1)} %get-tuple-element.701, f32[2,8,128]{2,1,0:T(8,128)S(1)} %get-tuple-element.702, f32[2,8,128]{2,1,0:T(8,128)S(1)} %get-tuple-element.699, f32[2,8,128]{2,1,0:T(8,128)S(1)} %get-tuple-element.698, ...), kind=kOutput, calls=%fused_computation.32.clone.1 | convolution fusion | flops 1705525248 | bytes 17467008 | tf_op jit(solution)/shard_map/while/body/eval_jaxpr/kgtn,nkd->kgtd/dot_general | solution.py:88
  824.6 7.8 fusion.78
  832.4 12.0 %fusion.79 = f32[2,8,128,128]{3,2,1,0:T(8,128)S(1)} fusion(f32[2,1601,128,8]{2,1,3,0:T(8,128)} %fusion.78, bf16[2,8,128,128]{3,2,1,0:T(8,128)(2,1)S(1)} %get-tuple-element.701, f32[2,8,128]{2,1,0:T(8,128)S(1)} %get-tuple-element.702, f32[2,8,128]{2,1,0:T(8,128)S(1)} %get-tuple-element.699, f32[2,8,128]{2,1,0:T(8,128)S(1)} %get-tuple-element.698, ...), kind=kOutput, calls=%fused_computation.32.clone.1 | convolution fusion | flops 1705525248 | bytes 17467008 | tf_op jit(solution)/shard_map/while/body/eval_jaxpr/kgtn,nkd->kgtd/dot_general | solution.py:88
  850.6 42.5 %all-gather.5.cloned.1.call-done = bf16[512,2048]{0,1:T(8,128)(2,1)} async-done(((bf16[128,2048]{0,1:T(8,128)(2,1)}), bf16[512,2048]{0,1:T(8,128)(2,1)}) %all-gather.5.cloned.1.call-update) | async-done | bytes 2097168 | tf_op jit(solution)/shard_map/all_gather | solution.py:139
  893.2 17.9 %fusion.42 = f32[2048,2048]{0,1:T(8,128)} fusion(bf16[512,2048]{0,1:T(8,128)(2,1)} %all-gather.5.cloned.1.call-done, bf16[512,2048]{1,0:T(8,128)(2,1)S(1)} %bitcast.136, f32[2048]{0:T(1024)S(1)} %copy-done.7, f32[2048,2048]{0,1:T(8,128)} %copy.62), kind=kOutput, calls=%fused_computation.47 | convolution fusion | flops 4357881856 | bytes 37756928 | tf_op jit(solution)/shard_map/dot_general | solution.py:137
  911.1 17.6 %copy.76 = f32[2048,2048]{1,0:T(8,128)} copy(f32[2048,2048]{0,1:T(8,128)} %fusion.42) | data formatting | bytes 33554432 | tf_op jit(solution)/shard_map/mul | solution.py:145
  (92 shorter events, 37.8 us)
Async XLA Ops:
  6.5 640.9 %all-gather.3.cloned.1.call-start = ((), (), s32[]{:S(2)}) async-start(), calls=%async_computation.1 | async-start | bytes 41943040 | tf_op jit(solution)/shard_map/all_gather | solution.py:120
  24.1 12.3 %copy-start.6 = (f32[2048]{0:T(1024)S(1)}, f32[2048]{0:T(1024)}, u32[]{:S(2)}) copy-start(f32[2048]{0:T(1024)} %param.16) | copy-start | bytes 24580
  36.4 14.0 %copy-start = (bf16[128,8192]{1,0:T(8,128)(2,1)S(1)}, bf16[128,8192]{1,0:T(8,128)(2,1)}, u32[]{:S(2)}) copy-start(bf16[128,8192]{1,0:T(8,128)(2,1)} %param.13) | copy-start | bytes 6291460
  50.4 8.9 copy-start.9
  52.9 794.8 %all-to-all-start = ((bf16[128,4,2048]{0,2,1:T(8,128)(2,1)}), bf16[128,4,2048]{0,2,1:T(8,128)(2,1)}, u32[]{:S(2)}, u32[]{:S(2)}) async-start(bf16[128,4,2048]{0,2,1:T(8,128)(2,1)} %bitcast.11), calls=%async_computation | async-start | bytes 4194304 | tf_op jit(solution)/shard_map/all_to_all | solution.py:117
  59.2 834.0 %all-gather.5.cloned.1.call-start = ((), (), s32[]{:S(2)}) async-start(), calls=%async_computation.2 | async-start | bytes 2621440 | tf_op jit(solution)/shard_map/all_gather | solution.py:139
  59.4 23.8 %copy-start.5 = (bf16[128,2048]{1,0:T(8,128)(2,1)S(1)}, bf16[128,2048]{1,0:T(8,128)(2,1)}, u32[]{:S(2)}) copy-start(bf16[128,2048]{1,0:T(8,128)(2,1)} %param.19) | copy-start | bytes 1572868
  59.4 24.4 %copy-start.8 = (s32[4]{0:T(128)S(1)}, s32[4]{0:T(128)}, u32[]{:S(2)}) copy-start(s32[4]{0:T(128)} %param.21) | copy-start | bytes 52
  664.9 15.2 %copy-start.3 = (f32[2,8,128,128]{3,2,1,0:T(8,128)S(1)}, f32[2,8,128,128]{3,2,1,0:T(8,128)}, u32[]{:S(2)}) copy-start(f32[2,8,128,128]{3,2,1,0:T(8,128)} %get-tuple-element.644) | copy-start | bytes 3145732 | tf_op jit(solution)/shard_map/while
  687.6 1.0 copy-start.4
  688.6 15.2 %copy-start.3 = (f32[2,8,128,128]{3,2,1,0:T(8,128)S(1)}, f32[2,8,128,128]{3,2,1,0:T(8,128)}, u32[]{:S(2)}) copy-start(f32[2,8,128,128]{3,2,1,0:T(8,128)} %get-tuple-element.644) | copy-start | bytes 3145732 | tf_op jit(solution)/shard_map/while
  711.2 1.0 copy-start.4
  712.2 15.2 %copy-start.3 = (f32[2,8,128,128]{3,2,1,0:T(8,128)S(1)}, f32[2,8,128,128]{3,2,1,0:T(8,128)}, u32[]{:S(2)}) copy-start(f32[2,8,128,128]{3,2,1,0:T(8,128)} %get-tuple-element.644) | copy-start | bytes 3145732 | tf_op jit(solution)/shard_map/while
  734.9 1.0 copy-start.4
  735.8 15.2 %copy-start.3 = (f32[2,8,128,128]{3,2,1,0:T(8,128)S(1)}, f32[2,8,128,128]{3,2,1,0:T(8,128)}, u32[]{:S(2)}) copy-start(f32[2,8,128,128]{3,2,1,0:T(8,128)} %get-tuple-element.644) | copy-start | bytes 3145732 | tf_op jit(solution)/shard_map/while
  758.5 1.0 copy-start.4
  761.7 131.5 %copy-start.7 = (f32[2048]{0:T(1024)S(1)}, f32[2048]{0:T(1024)}, u32[]{:S(2)}) copy-start(f32[2048]{0:T(1024)} %param.16) | copy-start | bytes 24580
  761.9 7.9 copy-start.1
  781.8 1.0 copy-start.2
  782.8 7.8 copy-start.1
  802.7 1.0 copy-start.2
  803.7 7.8 copy-start.1
  823.6 1.0 copy-start.2
  824.6 7.8 copy-start.1
  844.4 1.0 copy-start.2
Sparse Core Ops, SparseCore 0:
  50.5 596.9 all-gather.2
  847.8 45.3 all-gather.4
where the time goes:
time: 937 us; the launch traced here: 935 us
  waiting for transfers between devices  606 us (65%)
  matrix products  174 us (19%)
  local copies, waits for them, and re-layouts  90.2 us (10%)
  other arithmetic  44.4 us (5%)
  between operations  13.5 us (1%)
    all_gather x1, waiting for transfers between devices, per_device(): lax.all_gather(weight_q, 'text', axis=0, tiled=True)  563 us
    dot_general x8, matrix products, tile_of(): jnp.einsum('tkgd,nkd->kgtn', queries, keys_now, preferred_element_type=jn...  62.6 us
    unnamed x22, local copies, waits for them, and re-layouts  58 us
    dot_general x4, matrix products, backward(): jnp.einsum('kgtn,nkd->kgtd', score_grad, keys_now, preferred_element_type...  48.1 us
    all_gather x1, waiting for transfers between devices, per_device(): lax.all_gather(query_grad, 'text', axis=0, tiled=True)  42.5 us
    dot_general x4, matrix products, forward(): jnp.einsum('kgtn,nkd->kgtd', weights.astype(jnp.bfloat16), values_now, pr...  29.9 us
    reduce_sum x4, other arithmetic, forward(): total = total * fade + jnp.sum(weights, axis=-1)  29.2 us
  transfers between devices with their start and end apart: 3, of which 2 were waited for; matrix products, arithmetic and copies ran while one was open for 24% of the time, Pallas kernels for 0%

commit v1 on v0

--- a/solution.py
+++ b/solution.py
@@ -9,6 +9,28 @@
 IMAGES = 4
 IMG_TOK = 1601
 SPAN = 128
+
+
+def laid_out(blocks, dim):
+    blocks = jnp.moveaxis(blocks, 0, dim)
+    lengths = blocks.shape
+    return blocks.reshape(*lengths[:dim], lengths[dim] * lengths[dim + 1], *lengths[dim + 2 :])
+
+
+def collect(x, axis, dim):
+    size = lax.axis_size(axis)
+    pairs = [(i, (i + 1) % size) for i in range(size)]
+    back = [(b, a) for a, b in pairs]
+    lower, upper = ([], [])
+    for hop in range(size - 1):
+        if hop % 2 == 0:
+            lower.append(lax.ppermute(lower[-1] if lower else x, axis, pairs))
+        else:
+            upper.append(lax.ppermute(upper[-1] if upper else x, axis, back))
+    blocks = jnp.stack([*lower[::-1], x, *upper])
+    shift = lax.axis_index(axis) - len(lower)
+    blocks = blocks[(jnp.arange(size) - shift) % size]
+    return laid_out(blocks, dim)
 
 
 def visibility(span_ids, doc_images, image_start, total_spans):
@@ -115,11 +137,7 @@
         jnp.bfloat16
     )
     spread = lax.all_to_all(text_states, "text", split_axis=1, concat_axis=0, tiled=True)
-    q_sum = jnp.dot(
-        text_states,
-        lax.all_gather(weight_q, "text", axis=0, tiled=True),
-        preferred_element_type=jnp.float32,
-    )
+    q_sum = jnp.dot(text_states, collect(weight_q, "text", 0), preferred_element_type=jnp.float32)
     queries = q_sum.astype(jnp.bfloat16)
     first_token = lax.axis_index("text") * tok_dev
     span_ids = (first_token + jnp.arange(tok_dev, dtype=jnp.int32)) // SPAN

time: 937 us -> 1120 us (1.20)
  waiting for transfers between devices: 606 us -> 383 us
  starting transfers between devices: 6.32 us -> 187 us
  local copies, waits for them, and re-layouts: 90.2 us -> 259 us
  other arithmetic: 44.4 us -> 90.1 us
    all_gather x1 -> x0, waiting for transfers between devices: 563 us -> none  [per_device(): lax.all_gather(weight_q, 'text', axis=0, tiled=True)]
    ppermute x0 -> x3, waiting for transfers between devices: none -> 340 us  [the longest x2 340 us: collect(): lower.append(lax.ppermute(lower[-1] if lower else x, axis, pairs))]
    all_to_all x1, starting transfers between devices: 6.32 us -> 181 us  [per_device(): lax.all_to_all(text_states, 'text', split_axis=1, concat_axis=0, tiled=True)]
    gather x0 -> x65, local copies, waits for them, and re-layouts: none -> 163 us
    unnamed x4 -> x5, other arithmetic: 0.01 us -> 23 us
    another operation x1 -> x2, other arithmetic: 0.18 us -> 22.9 us  [the longest x1 22.7 us: collect(): blocks = jnp.stack([*lower[::-1], x, *upper])]
    unnamed x22 -> x34, local copies, waits for them, and re-layouts: 58 us -> 69 us
  transfers between devices with their start and end apart: 3 -> 5, of which waited for: 2 -> 3; matrix products, arithmetic and copies ran while one was open for 24% -> 40% of each run, Pallas kernels for 0% -> 0%
where the time goes in v1:
time: 1120 us; the launch traced here: 1110 us
  waiting for transfers between devices  383 us (34%)
  local copies, waits for them, and re-layouts  259 us (23%)
  starting transfers between devices  187 us (17%)
  matrix products  175 us (16%)
  other arithmetic  90.1 us (8%)
  between operations  13.9 us (1%)
    ppermute x2, waiting for transfers between devices, collect(): lower.append(lax.ppermute(lower[-1] if lower else x, axis, pairs))  340 us
    all_to_all x1, starting transfers between devices, per_device(): lax.all_to_all(text_states, 'text', split_axis=1, concat_axis=0, tiled=True)  181 us
    gather x64, local copies, waits for them, and re-layouts  140 us
    unnamed x34, local copies, waits for them, and re-layouts  69 us
    dot_general x8, matrix products, tile_of(): jnp.einsum('tkgd,nkd->kgtn', queries, keys_now, preferred_element_type=jn...  62.6 us
    dot_general x4, matrix products, backward(): jnp.einsum('kgtn,nkd->kgtd', score_grad, keys_now, preferred_element_type...  48.1 us
    all_gather x1, waiting for transfers between devices, per_device(): lax.all_gather(query_grad, 'text', axis=0, tiled=True)  43 us
    dot_general x4, matrix products, forward(): jnp.einsum('kgtn,nkd->kgtd', weights.astype(jnp.bfloat16), values_now, pr...  29.9 us
  transfers between devices with their start and end apart: 5, of which 3 were waited for; matrix products, arithmetic and copies ran while one was open for 40% of the time, Pallas kernels for 0%

profile of v1, /device:TPU:0, one launch (start us, length us, event | category | flops | bytes accessed | tf_op | source)
XLA Modules:
  0.0 1108.5 jit_solution(2086125572232701774)
XLA Ops:
  6.5 17.6 %copy.78 = f32[2048,2048]{0,1:T(8,128)} copy(f32[2048,2048]{1,0:T(8,128)} %param.15) | data formatting | bytes 33554432 | tf_op args[2]
  24.1 12.4 %copy.77 = bf16[2048,2048]{0,1:T(8,128)(2,1)} copy(bf16[2048,2048]{1,0:T(8,128)(2,1)} %param.14) | data formatting | bytes 16777216 | tf_op args[1]
  36.5 13.9 %multiply_convert_fusion = bf16[2048,2048]{0,1:T(8,128)(2,1)} fusion(bf16[2048,2048]{0,1:T(8,128)(2,1)} %copy.77, f32[2048]{0:T(1024)S(1)} %copy-done.8, f32[2048,2048]{0,1:T(8,128)} %copy.78), kind=kLoop, calls=%fused_computation.62 | loop fusion | flops 37748736 | bytes 33562624 | tf_op jit(solution)/shard_map/convert_element_type | solution.py:136
  55.5 181.6 %collective-permute-done = bf16[2048,2048]{0,1:T(8,128)(2,1)} collective-permute-done((bf16[2048,2048]{0,1:T(8,128)(2,1)}, bf16[2048,2048]{0,1:T(8,128)(2,1)}, u32[]{:S(2)}, u32[]{:S(2)}) %collective-permute-start) | collective-permute-done | bytes 8388640 | tf_op jit(solution)/shard_map/ppermute | solution.py:27
  239.6 181.5 %all-to-all-start = ((bf16[128,4,2048]{0,2,1:T(8,128)(2,1)}), bf16[128,4,2048]{0,2,1:T(8,128)(2,1)}, u32[]{:S(2)}, u32[]{:S(2)}) async-start(bf16[128,4,2048]{0,2,1:T(8,128)(2,1)} %bitcast.16), calls=%async_computation | async-start | bytes 4194304 | tf_op jit(solution)/shard_map/all_to_all | solution.py:139
  440.1 158.5 %collective-permute-done.1 = bf16[2048,2048]{0,1:T(8,128)(2,1)} collective-permute-done((bf16[2048,2048]{0,1:T(8,128)(2,1)}, bf16[2048,2048]{0,1:T(8,128)(2,1)}, u32[]{:S(2)}, u32[]{:S(2)}) %collective-permute-start.1) | collective-permute-done | bytes 8388640 | tf_op jit(solution)/shard_map/ppermute | solution.py:27
  598.6 22.7 %pad_maximum_fusion = bf16[4,2048,2048]{1,2,0:T(8,128)(2,1)} fusion(bf16[1,2048,2048]{1,2,0:T(8,128)(2,1)} %bitcast.6, bf16[1,2048,2048]{1,2,0:T(8,128)(2,1)} %bitcast.5, bf16[1,2048,2048]{1,2,0:T(8,128)(2,1)} %bitcast.4, bf16[1,2048,2048]{1,2,0:T(8,128)(2,1)} %bitcast.3), kind=kLoop, calls=%fused_computation.57 | loop fusion | flops 50331648 | bytes 67108864 | tf_op jit(solution)/shard_map/stack | solution.py:30
  621.3 23.2 %fusion.48 = (bf16[4,512,2048]{1,2,0:T(8,128)(2,1)}, bf16[4,512,2048]{1,2,0:T(8,128)(2,1)}, bf16[4,512,2048]{1,2,0:T(8,128)(2,1)}, bf16[4,512,2048]{1,2,0:T(8,128)(2,1)}) fusion(bf16[4,2048,2048]{1,2,0:T(8,128)(2,1)} %pad_maximum_fusion), kind=kLoop, calls=%fused_computation.90 | loop fusion | bytes 67108864 | tf_op jit(solution)/shard_map/gather | solution.py:32
  648.7 34.9 %while.36 = (s32[]{:T(128)}, bf16[4,512,2048]{1,2,0:T(8,128)(2,1)}, s32[4,1]{0,1:T(1,128)S(1)}, bf16[4,512,2048]{2,1,0:T(8,128)(2,1)}, s32[]{:T(128)}) while((s32[]{:T(128)}, bf16[4,512,2048]{1,2,0:T(8,128)(2,1)}, s32[4,1]{0,1:T(1,128)S(1)}, bf16[4,512,2048]{2,1,0:T(8,128)(2,1)}, s32[]{:T(128)}) %tuple.152), condition=%wide.while_cond, body=%wide.while_body.sunk | while | flops 2 | bytes 12583501 | solution.py:32
  688.0 34.9 %while.37 = (s32[]{:T(128)}, bf16[4,512,2048]{1,2,0:T(8,128)(2,1)}, s32[4,1]{0,1:T(1,128)S(1)}, bf16[4,512,2048]{2,1,0:T(8,128)(2,1)}, s32[]{:T(128)}) while((s32[]{:T(128)}, bf16[4,512,2048]{1,2,0:T(8,128)(2,1)}, s32[4,1]{0,1:T(1,128)S(1)}, bf16[4,512,2048]{2,1,0:T(8,128)(2,1)}, s32[]{:T(128)}) %tuple.170), condition=%wide.while_cond.1, body=%wide.while_body.1.sunk | while | flops 2 | bytes 12583501 | solution.py:32
  727.2 34.9 %while.38 = (s32[]{:T(128)}, bf16[4,512,2048]{1,2,0:T(8,128)(2,1)}, s32[4,1]{0,1:T(1,128)S(1)}, bf16[4,512,2048]{2,1,0:T(8,128)(2,1)}, s32[]{:T(128)}) while((s32[]{:T(128)}, bf16[4,512,2048]{1,2,0:T(8,128)(2,1)}, s32[4,1]{0,1:T(1,128)S(1)}, bf16[4,512,2048]{2,1,0:T(8,128)(2,1)}, s32[]{:T(128)}) %tuple.171), condition=%wide.while_cond.2, body=%wide.while_body.2.sunk | while | flops 2 | bytes 12583501 | solution.py:32
  766.4 34.9 %while.39 = (s32[]{:T(128)}, bf16[4,512,2048]{1,2,0:T(8,128)(2,1)}, s32[4,1]{0,1:T(1,128)S(1)}, bf16[4,512,2048]{2,1,0:T(8,128)(2,1)}, s32[]{:T(128)}) while((s32[]{:T(128)}, bf16[4,512,2048]{1,2,0:T(8,128)(2,1)}, s32[4,1]{0,1:T(1,128)S(1)}, bf16[4,512,2048]{2,1,0:T(8,128)(2,1)}, s32[]{:T(128)}) %tuple.172), condition=%wide.while_cond.3, body=%wide.while_body.3.sunk | while | flops 2 | bytes 12583501 | solution.py:32
  801.3 23.0 %pad_maximum_fusion.1 = bf16[4,2048,2048]{2,1,0:T(8,128)(2,1)} fusion(bf16[4,512,2048]{2,1,0:T(8,128)(2,1)} %get-tuple-element.350, bf16[4,512,2048]{2,1,0:T(8,128)(2,1)} %get-tuple-element.342, bf16[4,512,2048]{2,1,0:T(8,128)(2,1)} %get-tuple-element.334, bf16[4,512,2048]{2,1,0:T(8,128)(2,1)} %get-tuple-element.326), kind=kLoop, calls=%fused_computation.58 | loop fusion | flops 134217728 | bytes 67108864
  824.3 16.5 %convolution_convert_fusion = bf16[2048,128]{1,0:T(8,128)(2,1)} fusion(bf16[8192,2048]{1,0:T(8,128)(2,1)} %bitcast.149, bf16[128,8192]{1,0:T(8,128)(2,1)S(1)} %copy-done.2), kind=kOutput, calls=%fused_computation.64 | convolution fusion | flops 4295229440 | bytes 36175872 | tf_op jit(solution)/shard_map/dot_general | solution.py:140
  842.2 90.8 %while.40 = (s32[]{:T(128)}, f32[2,8,128]{2,1,0:T(8,128)S(1)}, f32[2,8,128]{2,1,0:T(8,128)S(1)}, f32[2,8,128,128]{3,2,1,0:T(8,128)S(1)}, pred[128,4]{0,1:T(4,128...) while((s32[]{:T(128)}, f32[2,8,128]{2,1,0:T(8,128)S(1)}, ...), condition=%wide.region_7.8_spmd.clone, body=%wide.region_4.7_spmd.clone.sunk | while | flops 1712357376 | bytes 43803448 | solution.py:93
  842.2 7.8 bitcast_reduce_fusion.2
  857.4 7.5 fusion.74
  864.9 7.8 bitcast_reduce_fusion.2
  887.6 7.8 bitcast_reduce_fusion.2
  910.2 7.8 bitcast_reduce_fusion.2
  934.1 83.5 %while.41 = (s32[]{:T(128)}, f32[2,8,128,128]{3,2,1,0:T(8,128)}, pred[128,4]{0,1:T(4,128)(4,1)S(1)}, bf16[6404,2,128]{2,0,1:T(8,128)(2,1)}, bf16[128,2,8,128]{3,...) while((s32[]{:T(128)}, f32[2,8,128,128]{3,2,1,0:T(8,128)}, ...), condition=%wide.region_10.11_spmd.clone, body=%wide.region_9.10_spmd.clone.sunk | while | flops 2544910336 | bytes 40319100 | solution.py:114
  934.1 7.9 fusion.80
  942.0 12.0 %fusion.81 = f32[2,8,128,128]{3,2,1,0:T(8,128)S(1)} fusion(f32[2,1601,128,8]{2,1,3,0:T(8,128)} %fusion.80, bf16[2,8,128,128]{3,2,1,0:T(8,128)(2,1)S(1)} %get-tuple-element.1009, f32[2,8,128]{2,1,0:T(8,128)S(1)} %get-tuple-element.1010, f32[2,8,128]{2,1,0:T(8,128)S(1)} %get-tuple-element.1007, f32[2,8,128]{2,1,0:T(8,128)S(1)} %get-tuple-element.1006, ...), kind=kOutput, calls=%fused_computation.44.clone.1 | convolution fusion | flops 1705525248 | bytes 17467008 | tf_op jit(solution)/shard_map/while/body/eval_jaxpr/kgtn,nkd->kgtd/dot_general | solution.py:110
  955.0 7.9 fusion.80
  962.8 12.0 %fusion.81 = f32[2,8,128,128]{3,2,1,0:T(8,128)S(1)} fusion(f32[2,1601,128,8]{2,1,3,0:T(8,128)} %fusion.80, bf16[2,8,128,128]{3,2,1,0:T(8,128)(2,1)S(1)} %get-tuple-element.1009, f32[2,8,128]{2,1,0:T(8,128)S(1)} %get-tuple-element.1010, f32[2,8,128]{2,1,0:T(8,128)S(1)} %get-tuple-element.1007, f32[2,8,128]{2,1,0:T(8,128)S(1)} %get-tuple-element.1006, ...), kind=kOutput, calls=%fused_computation.44.clone.1 | convolution fusion | flops 1705525248 | bytes 17467008 | tf_op jit(solution)/shard_map/while/body/eval_jaxpr/kgtn,nkd->kgtd/dot_general | solution.py:110
  975.8 7.9 fusion.80
  983.7 12.0 %fusion.81 = f32[2,8,128,128]{3,2,1,0:T(8,128)S(1)} fusion(f32[2,1601,128,8]{2,1,3,0:T(8,128)} %fusion.80, bf16[2,8,128,128]{3,2,1,0:T(8,128)(2,1)S(1)} %get-tuple-element.1009, f32[2,8,128]{2,1,0:T(8,128)S(1)} %get-tuple-element.1010, f32[2,8,128]{2,1,0:T(8,128)S(1)} %get-tuple-element.1007, f32[2,8,128]{2,1,0:T(8,128)S(1)} %get-tuple-element.1006, ...), kind=kOutput, calls=%fused_computation.44.clone.1 | convolution fusion | flops 1705525248 | bytes 17467008 | tf_op jit(solution)/shard_map/while/body/eval_jaxpr/kgtn,nkd->kgtd/dot_general | solution.py:110
  996.7 7.9 fusion.80
  1004.6 12.0 %fusion.81 = f32[2,8,128,128]{3,2,1,0:T(8,128)S(1)} fusion(f32[2,1601,128,8]{2,1,3,0:T(8,128)} %fusion.80, bf16[2,8,128,128]{3,2,1,0:T(8,128)(2,1)S(1)} %get-tuple-element.1009, f32[2,8,128]{2,1,0:T(8,128)S(1)} %get-tuple-element.1010, f32[2,8,128]{2,1,0:T(8,128)S(1)} %get-tuple-element.1007, f32[2,8,128]{2,1,0:T(8,128)S(1)} %get-tuple-element.1006, ...), kind=kOutput, calls=%fused_computation.44.clone.1 | convolution fusion | flops 1705525248 | bytes 17467008 | tf_op jit(solution)/shard_map/while/body/eval_jaxpr/kgtn,nkd->kgtd/dot_general | solution.py:110
  1022.8 43.0 %all-gather.2.cloned.1.call-done = bf16[512,2048]{0,1:T(8,128)(2,1)} async-done(((bf16[128,2048]{0,1:T(8,128)(2,1)}), bf16[512,2048]{0,1:T(8,128)(2,1)}) %all-gather.2.cloned.1.call-update) | async-done | bytes 2097168 | tf_op jit(solution)/shard_map/all_gather | solution.py:157
  1065.8 18.1 %fusion.42 = f32[2048,2048]{0,1:T(8,128)} fusion(bf16[512,2048]{0,1:T(8,128)(2,1)} %all-gather.2.cloned.1.call-done, bf16[512,2048]{1,0:T(8,128)(2,1)S(1)} %bitcast.154, f32[2048]{0:T(1024)S(1)} %copy-done.9, f32[2048,2048]{0,1:T(8,128)} %copy.78), kind=kOutput, calls=%fused_computation.61 | convolution fusion | flops 4357881856 | bytes 37756928 | tf_op jit(solution)/shard_map/dot_general | solution.py:155
  1083.9 17.6 %copy.96 = f32[2048,2048]{1,0:T(8,128)} copy(f32[2048,2048]{0,1:T(8,128)} %fusion.42) | data formatting | bytes 33554432 | tf_op jit(solution)/shard_map/mul | solution.py:163
  (163 shorter events, 246.4 us)
Async XLA Ops:
  24.1 12.4 %copy-start.8 = (f32[2048]{0:T(1024)S(1)}, f32[2048]{0:T(1024)}, u32[]{:S(2)}) copy-start(f32[2048]{0:T(1024)} %param.16) | copy-start | bytes 24580
  36.5 200.6 %copy-start.1 = (bf16[128,8192]{1,0:T(8,128)(2,1)S(1)}, bf16[128,8192]{1,0:T(8,128)(2,1)}, u32[]{:S(2)}) copy-start(bf16[128,8192]{1,0:T(8,128)(2,1)} %param.13) | copy-start | bytes 6291460
  50.4 371.0 %copy-start.11 = (s32[3]{0:T(128)S(1)}, s32[3]{0:T(128)}, u32[]{:S(2)}) copy-start(s32[3]{0:T(128)} %param.20) | copy-start | bytes 40
  50.4 186.7 %collective-permute-start = (bf16[2048,2048]{0,1:T(8,128)(2,1)}, bf16[2048,2048]{0,1:T(8,128)(2,1)}, u32[]{:S(2)}, u32[]{:S(2)}) collective-permute-start(bf16[2048,2048]{0,1:T(8,128)(2,1)} %multiply_convert_fusion), channel_id=1, source_target_pairs={{0,4},{4,8},{8,12},{12,0},{1,5},{5,9},{9,13},{13,1},{2,6},{6,10},{... | collective-permute-start | bytes 25165832 | tf_op jit(solution)/shard_map/ppermute | solution.py:27
  53.5 386.7 %collective-permute-start.2 = (bf16[2048,2048]{0,1:T(8,128)(2,1)}, bf16[2048,2048]{0,1:T(8,128)(2,1)}, u32[]{:S(2)}, u32[]{:S(2)}) collective-permute-start(bf16[2048,2048]{0,1:T(8,128)(2,1)} %multiply_convert_fusion), channel_id=1, source_target_pairs={{4,0},{8,4},{12,8},{0,12},{5,1},{9,5},{13,9},{1,13},{6,2},{10,6},{... | collective-permute-start | bytes 25165832 | tf_op jit(solution)/shard_map/ppermute | solution.py:29
  237.1 361.5 %collective-permute-start.1 = (bf16[2048,2048]{0,1:T(8,128)(2,1)}, bf16[2048,2048]{0,1:T(8,128)(2,1)}, u32[]{:S(2)}, u32[]{:S(2)}) collective-permute-start(bf16[2048,2048]{0,1:T(8,128)(2,1)} %collective-permute-done), channel_id=1, source_target_pairs={{0,4},{4,8},{8,12},{12,0},{1,5},{5,9},{9,13},{13,1},{2,6},{6,10},{... | collective-permute-start | bytes 25165832 | tf_op jit(solution)/shard_map/ppermute | solution.py:27
  239.6 780.3 %all-to-all-start = ((bf16[128,4,2048]{0,2,1:T(8,128)(2,1)}), bf16[128,4,2048]{0,2,1:T(8,128)(2,1)}, u32[]{:S(2)}, u32[]{:S(2)}) async-start(bf16[128,4,2048]{0,2,1:T(8,128)(2,1)} %bitcast.16), calls=%async_computation | async-start | bytes 4194304 | tf_op jit(solution)/shard_map/all_to_all | solution.py:139
  421.1 644.7 %all-gather.2.cloned.1.call-start = ((), (), s32[]{:S(2)}) async-start(), calls=%async_computation.1 | async-start | bytes 2621440 | tf_op jit(solution)/shard_map/all_gather | solution.py:157
  429.5 10.3 copy-start.10
  801.3 23.0 %copy-start.2 = (bf16[128,8192]{1,0:T(8,128)(2,1)S(1)}, bf16[128,8192]{1,0:T(8,128)(2,1)}, u32[]{:S(2)}) copy-start(bf16[128,8192]{1,0:T(8,128)(2,1)} %param.13) | copy-start | bytes 6291460
  824.3 17.9 %copy-start.5 = (f32[2,8,128,128]{3,2,1,0:T(8,128)S(1)}, f32[2,8,128,128]{3,2,1,0:T(8,128)}, u32[]{:S(2)}) copy-start(f32[2,8,128,128]{3,2,1,0:T(8,128)} %custom-call.2) | copy-start | bytes 3145732
  824.3 17.9 %copy-start.6 = (f32[2,8,128]{2,1,0:T(8,128)S(1)}, f32[2,8,128]{2,1,0:T(8,128)}, u32[]{:S(2)}) copy-start(f32[2,8,128]{2,1,0:T(8,128)} %custom-call) | copy-start | bytes 24580
  824.3 17.9 %copy-start.7 = (f32[2,8,128]{2,1,0:T(8,128)S(1)}, f32[2,8,128]{2,1,0:T(8,128)}, u32[]{:S(2)}) copy-start(f32[2,8,128]{2,1,0:T(8,128)} %custom-call.1) | copy-start | bytes 24580
  842.2 91.2 %copy-start = (bf16[128,2048]{0,1:T(8,128)(2,1)S(1)}, bf16[128,2048]{0,1:T(8,128)(2,1)}, u32[]{:S(2)}) copy-start(bf16[128,2048]{0,1:T(8,128)(2,1)} %copy.88) | copy-start | bytes 1572868
  934.0 131.8 %copy-start.9 = (f32[2048]{0:T(1024)S(1)}, f32[2048]{0:T(1024)}, u32[]{:S(2)}) copy-start(f32[2048]{0:T(1024)} %param.16) | copy-start | bytes 24580
  934.1 7.9 copy-start.3
  954.0 1.0 copy-start.4
  955.0 7.9 copy-start.3
  974.9 1.0 copy-start.4
  975.8 7.9 copy-start.3
  995.7 1.0 copy-start.4
  996.7 7.9 copy-start.3
  1016.6 1.0 copy-start.4
Sparse Core Ops, SparseCore 0:
  1020.0 45.7 all-gather.1
